TPU v7x, 256 devices: a whole 4x4x8 slice. The times are simulated.
256 devices in a mesh: seq: 32 (over y, z), head: 8 (over x, core).
Axes of the slice: x: 4, y: 4, z: 8, core: 2. Of those that a mesh axis runs over, the one named last changes fastest.
Arguments:
- tokens: bfloat16 [32768, 4096], P('seq'), may hold values from -50 to 50
- norm_gain: float32 [4096], replicated, may hold values from 0.1 to 1.9
- wq: bfloat16 [4096, 4096], P('seq', 'head'), may hold values from -2.34375 to 2.34375
- wk: bfloat16 [4096, 1024], P('seq', 'head'), may hold values from -0.09375 to 0.09375
- wv: bfloat16 [4096, 1024], P('seq', 'head'), may hold values from -0.09375 to 0.09375
- wo: bfloat16 [4096, 4096], P('head', 'seq'), may hold values from -0.1875 to 0.1875
- gate_bias: float32 [32], P('head'), may hold values from -3 to 3
- mem_init: float32 [8, 128, 128], P('head'), may hold values from -32768 to 32768
- norm_init: float32 [8, 128], P('head'), may hold values from 512 to 2048
Outputs:
- attended: bfloat16 [32768, 4096], P('seq', 'head')
All inputs are finite; a program needn't handle non-finite values.
Results may differ from a plain program's by a relative error of at most 0.018.
Values may be sent and summed in bfloat16 or wider, within the bound.
No kernel may reach another device: no remote copies, remote signals or barrier semaphores. Data moves between devices by JAX's collectives and lax.ppermute only.
A program may use at most 128 MiB of HBM per device.

v0:
```python
import math
import jax
import jax.numpy as jnp
from jax import lax
from jax.sharding import PartitionSpec as P

H = 32
KVH = 8
HD = 128
SEG = 512


def from_behind(block, axis, distance):
    devices = range(lax.axis_size(axis))
    route = [(i - distance, i) for i in devices if i - distance in devices]
    return lax.ppermute(block, axis, route)


def feature_map(values_in):
    return jnp.where(values_in > 0, values_in + 1.0, jnp.exp(jnp.minimum(values_in, 0.0)))


def per_device(tokens, norm_gain, wq, wk, wv, wo, gate_bias, mem_init, norm_init):
    highest = lax.Precision.HIGHEST
    widened = tokens.astype(jnp.float32)
    normed = (
        widened * lax.rsqrt(jnp.mean(widened * widened, axis=-1, keepdims=True) + 1e-05) * norm_gain
    ).astype(jnp.bfloat16)
    token_count = normed.shape[0]

    def project(shard_piece):
        return jnp.dot(normed, shard_piece, preferred_element_type=jnp.float32)

    query_wide = project(lax.all_gather(wq, "seq", axis=0, tiled=True))
    key_wide = project(lax.all_gather(wk, "seq", axis=0, tiled=True))
    value_wide = project(lax.all_gather(wv, "seq", axis=0, tiled=True))
    queries = query_wide.astype(jnp.bfloat16)
    keys_all = key_wide.astype(jnp.bfloat16)
    values_all = value_wide.astype(jnp.bfloat16)
    group = H // KVH
    kv_local = wk.shape[1] // HD
    segments = token_count // SEG
    query_seg = queries.reshape(segments, SEG, kv_local, group, HD)
    key_seg = keys_all.reshape(segments, SEG, kv_local, HD)
    value_seg = values_all.reshape(segments, SEG, kv_local, HD)
    key_feats = feature_map(key_seg.astype(jnp.float32))
    delta_mem = jnp.einsum(
        "nski,nskj->nkij", key_feats, value_seg.astype(jnp.float32), precision=highest
    )
    delta_norm = jnp.sum(key_feats, axis=1)
    own_mem = jnp.sum(delta_mem, axis=0)
    own_norm = jnp.sum(delta_norm, axis=0)
    zero_mem = jnp.zeros_like(own_mem)
    zero_norm = jnp.zeros_like(own_norm)

    def pass_along(step_index, carried):
        return (
            from_behind((carried[0] + own_mem).astype(jnp.bfloat16), "seq", 1).astype(jnp.float32),
            from_behind((carried[1] + own_norm).astype(jnp.bfloat16), "seq", 1).astype(jnp.float32),
        )

    carried_mem, carried_norm = lax.fori_loop(
        0, lax.axis_size("seq") - 1, pass_along, (zero_mem, zero_norm)
    )
    inner_mem = jnp.concatenate([zero_mem[None], jnp.cumsum(delta_mem, axis=0)[:-1]], axis=0)
    inner_norm = jnp.concatenate([zero_norm[None], jnp.cumsum(delta_norm, axis=0)[:-1]], axis=0)
    mem_before = mem_init[None] + carried_mem[None] + inner_mem
    norm_before = norm_init[None] + carried_norm[None] + inner_norm
    query_feats = feature_map(query_seg.astype(jnp.float32))
    numer = jnp.einsum("nskgi,nkij->nskgj", query_feats, mem_before, precision=highest)
    denom = jnp.einsum("nskgi,nki->nskg", query_feats, norm_before, precision=highest)
    retrieved = numer / denom[..., None]
    score_scale = 1.0 / math.sqrt(HD)
    causal = lax.broadcasted_iota(jnp.int32, (SEG, SEG), 0) >= lax.broadcasted_iota(
        jnp.int32, (SEG, SEG), 1
    )
    scores = (
        jnp.einsum("nqkgd,nskd->nkgqs", query_seg, key_seg, preferred_element_type=jnp.float32)
        * score_scale
    )
    scores = jnp.where(causal, scores, -1e30)
    peak = jnp.max(scores, axis=-1, keepdims=True)
    expd = jnp.exp(scores - peak)
    probs = (expd / jnp.sum(expd, axis=-1, keepdims=True)).astype(jnp.bfloat16)
    local = jnp.einsum("nkgqs,nskd->nqkgd", probs, value_seg, preferred_element_type=jnp.float32)
    gate_mix = jax.nn.sigmoid(gate_bias).reshape(kv_local, group)
    mixed = (
        gate_mix[None, None, :, :, None] * retrieved
        + (1.0 - gate_mix)[None, None, :, :, None] * local
    )
    mixed = mixed.astype(jnp.bfloat16).reshape(token_count, kv_local * group * HD)
    partial_out = jnp.dot(
        mixed, lax.all_gather(wo, "seq", axis=1, tiled=True), preferred_element_type=jnp.float32
    )
    return lax.psum_scatter(
        partial_out.astype(jnp.bfloat16), "head", scatter_dimension=1, tiled=True
    )


def solution(mesh):
    placed = (
        P("seq", None),
        P(),
        P("seq", "head"),
        P("seq", "head"),
        P("seq", "head"),
        P("head", "seq"),
        P("head"),
        P("head", None, None),
        P("head", None),
    )
    return jax.shard_map(
        per_device, mesh=mesh, in_specs=placed, out_specs=P("seq", "head"), check_vma=False
    )
```

profile of v0, /device:TPU:1, one launch (start us, length us, event | category | flops | bytes accessed | tf_op | source)
XLA Modules:
  0.0 559.1 jit_solution(2536971388080526449)
XLA Ops:
  9.5 5.1 fusion.3
  15.2 10.3 %fusion.5 = bf16[1024,4096]{1,0:T(8,128)(2,1)} fusion(bf16[1024,4096]{1,0:T(8,128)(2,1)} %param.11, f32[4096]{0:T(1024)S(1)} %copy-done.2, f32[1024]{0:T(1024)S(1)} %add_rsqrt_fusion), kind=kLoop, calls=%fused_computation.9 | loop fusion | flops 16777216 | bytes 16797696 | tf_op jit(solution)/shard_map/convert_element_type | solution.py:28
  25.5 60.1 %all-gather.5.cloned.1.call-done = bf16[4096,128]{1,0:T(8,128)(2,1)} async-done(((bf16[128,128]{1,0:T(8,128)(2,1)}), bf16[4096,128]{1,0:T(8,128)(2,1)}) %all-gather.5.cloned.1.call-update) | async-done | bytes 1048592 | tf_op jit(solution)/shard_map/all_gather | solution.py:35
  85.6 6.0 %fusion.38 = (f32[128]{0:T(128)S(1)}, bf16[1024,128]{1,0:T(8,128)(2,1)S(1)}) fusion(bf16[1024,4096]{1,0:T(8,128)(2,1)} %fusion.5, bf16[4096,128]{1,0:T(8,128)(2,1)} %all-gather.5.cloned.1.call-done), kind=kOutput, calls=%fused_computation.57 | convolution fusion | flops 1074659200 | bytes 9699840 | tf_op jit(solution)/shard_map/dot_general | solution.py:32
  91.7 70.3 %all-gather.7.cloned.1.call-done = bf16[4096,128]{1,0:T(8,128)(2,1)} async-done(((bf16[128,128]{1,0:T(8,128)(2,1)}), bf16[4096,128]{1,0:T(8,128)(2,1)}) %all-gather.7.cloned.1.call-update) | async-done | bytes 1048592 | tf_op jit(solution)/shard_map/all_gather | solution.py:36
  162.0 5.9 %convolution_convert_fusion.2 = bf16[1024,128]{1,0:T(8,128)(2,1)S(1)} fusion(bf16[1024,4096]{1,0:T(8,128)(2,1)} %fusion.5, bf16[4096,128]{1,0:T(8,128)(2,1)} %all-gather.7.cloned.1.call-done), kind=kOutput, calls=%fused_computation.32 | convolution fusion | flops 1073872896 | bytes 9699328 | tf_op jit(solution)/shard_map/dot_general | solution.py:32
  168.9 253.9 %while.13 = (s32[]{:T(128)}, f32[1,128,128]{2,1,0:T(8,128)S(1)}, f32[1,128]{1,0:T(1,128)S(1)}, f32[1,128,128]{2,1,0:T(8,128)S(1)}, f32[1,128]{1,0:T(1,128)S(1)}, /*index=5*/s32[]{:T(128)}, s32[]{:T(128)}) while((s32[]{:T(128)}, f32[1,128,128]{2,1,0:T(8,128)S(1)}, f32[1,128]{1,0:T(1,128)S(1)}, f32[1,128,128]{2,1,0:T(8,128)S(1)}, ...), condition=%wide.region_4.5_spmd.clone, body=%wide.region_3.4_spmd.clone.sunk | while | flops 66051 | bytes 396456 | solution.py:62
  171.1 4.0 collective-permute-start.1
  182.2 4.0 collective-permute-start
  197.8 4.0 collective-permute-start
  221.2 4.0 collective-permute-start
  229.8 4.0 collective-permute-start
  233.8 4.0 collective-permute-start.1
  238.5 4.0 collective-permute-start
  246.9 4.0 collective-permute-start
  279.8 4.0 collective-permute-start
  292.2 4.0 collective-permute-start.1
  305.1 4.0 collective-permute-start
  313.5 4.0 collective-permute-start
  317.5 4.1 collective-permute-start.1
  322.4 4.0 collective-permute-start
  330.8 4.0 collective-permute-start
  334.8 4.4 collective-permute-start.1
  340.0 4.0 collective-permute-start
  367.7 4.3 collective-permute-start.1
  384.6 4.1 collective-permute-start.1
  401.3 4.0 collective-permute-start.1
  409.7 4.0 collective-permute-start.1
  418.1 4.0 collective-permute-start.1
  422.9 9.0 %convolution_convert_fusion.1 = bf16[1024,512]{1,0:T(8,128)(2,1)S(1)} fusion(bf16[1024,4096]{1,0:T(8,128)(2,1)} %fusion.5, bf16[4096,512]{1,0:T(8,128)(2,1)} %all-gather.9.cloned.1.call-done), kind=kOutput, calls=%fused_computation.31 | convolution fusion | flops 4295491584 | bytes 13631488 | tf_op jit(solution)/shard_map/dot_general | solution.py:32
  445.5 8.9 %convolution_convert_fusion = bf16[1024,4096]{1,0:T(8,128)(2,1)} fusion(bf16[512,4096]{1,0:T(8,128)(2,1)} %all-gather.11.cloned.1.call-done, bf16[128,8,4,128]{3,2,1,0:T(4,128)(2,1)S(1)} %bitcast.93), kind=kOutput, calls=%fused_computation.13 | convolution fusion | flops 4299161600 | bytes 13631488 | tf_op jit(solution)/shard_map/dot_general | solution.py:92
  454.5 98.1 %reduce-scatter.2.cloned.1.call-done = bf16[1024,512]{1,0:T(8,128)(2,1)} async-done(((bf16[1024,4096]{1,0:T(8,128)(2,1)}), bf16[1024,512]{1,0:T(8,128)(2,1)}) %reduce-scatter.2.cloned.1.call-update) | async-done | bytes 1048592 | tf_op jit(solution)/shard_map/reduce_scatter | solution.py:95
  (277 shorter events, 181.8 us)
Async XLA Ops:
  6.5 79.0 %all-gather.5.cloned.1.call-start = ((), (), s32[]{:S(2)}) async-start(), calls=%async_computation.1 | async-start | bytes 1081344 | tf_op jit(solution)/shard_map/all_gather | solution.py:35
  7.3 154.7 %all-gather.7.cloned.1.call-start = ((), (), s32[]{:S(2)}) async-start(), calls=%async_computation.2 | async-start | bytes 1081344 | tf_op jit(solution)/shard_map/all_gather | solution.py:36
  8.0 414.9 %all-gather.9.cloned.1.call-start = ((), (), s32[]{:S(2)}) async-start(), calls=%async_computation.3 | async-start | bytes 4325376 | tf_op jit(solution)/shard_map/all_gather | solution.py:34
  8.7 436.8 %all-gather.11.cloned.1.call-start = ((), (), s32[]{:S(2)}) async-start(), calls=%async_computation.4 | async-start | bytes 4325376 | tf_op jit(solution)/shard_map/all_gather | solution.py:93
  9.3 543.3 %reduce-scatter.2.cloned.1.call-start = ((), (), s32[]{:S(2)}) async-start(), calls=%async_computation.5 | async-start | bytes 9437184 | tf_op jit(solution)/shard_map/reduce_scatter | solution.py:95
  182.2 8.1 %collective-permute-start = (bf16[1,128,128]{2,1,0:T(8,128)(2,1)S(1)}, bf16[1,128,128]{2,1,0:T(8,128)(2,1)S(1)}, u32[]{:S(2)}, u32[]{:S(2)}) collective-permute-start(bf16[1,128,128]{2,1,0:T(8,128)(2,1)S(1)} %fusion.74), channel_id=1, source_target_pairs={{0,8},{8,16},{16,24},{24,32},{32,40},{40,48},{48,56},{56,64},{64,7... | collective-permute-start | bytes 98312 | tf_op jit(solution)/shard_map/while/body/eval_jaxpr/ppermute | solution.py:16
  197.8 8.1 %collective-permute-start = (bf16[1,128,128]{2,1,0:T(8,128)(2,1)S(1)}, bf16[1,128,128]{2,1,0:T(8,128)(2,1)S(1)}, u32[]{:S(2)}, u32[]{:S(2)}) collective-permute-start(bf16[1,128,128]{2,1,0:T(8,128)(2,1)S(1)} %fusion.74), channel_id=1, source_target_pairs={{0,8},{8,16},{16,24},{24,32},{32,40},{40,48},{48,56},{56,64},{64,7... | collective-permute-start | bytes 98312 | tf_op jit(solution)/shard_map/while/body/eval_jaxpr/ppermute | solution.py:16
  205.9 7.8 %collective-permute-start = (bf16[1,128,128]{2,1,0:T(8,128)(2,1)S(1)}, bf16[1,128,128]{2,1,0:T(8,128)(2,1)S(1)}, u32[]{:S(2)}, u32[]{:S(2)}) collective-permute-start(bf16[1,128,128]{2,1,0:T(8,128)(2,1)S(1)} %fusion.74), channel_id=1, source_target_pairs={{0,8},{8,16},{16,24},{24,32},{32,40},{40,48},{48,56},{56,64},{64,7... | collective-permute-start | bytes 98312 | tf_op jit(solution)/shard_map/while/body/eval_jaxpr/ppermute | solution.py:16
  221.2 8.5 %collective-permute-start = (bf16[1,128,128]{2,1,0:T(8,128)(2,1)S(1)}, bf16[1,128,128]{2,1,0:T(8,128)(2,1)S(1)}, u32[]{:S(2)}, u32[]{:S(2)}) collective-permute-start(bf16[1,128,128]{2,1,0:T(8,128)(2,1)S(1)} %fusion.74), channel_id=1, source_target_pairs={{0,8},{8,16},{16,24},{24,32},{32,40},{40,48},{48,56},{56,64},{64,7... | collective-permute-start | bytes 98312 | tf_op jit(solution)/shard_map/while/body/eval_jaxpr/ppermute | solution.py:16
  229.8 8.7 %collective-permute-start = (bf16[1,128,128]{2,1,0:T(8,128)(2,1)S(1)}, bf16[1,128,128]{2,1,0:T(8,128)(2,1)S(1)}, u32[]{:S(2)}, u32[]{:S(2)}) collective-permute-start(bf16[1,128,128]{2,1,0:T(8,128)(2,1)S(1)} %fusion.74), channel_id=1, source_target_pairs={{0,8},{8,16},{16,24},{24,32},{32,40},{40,48},{48,56},{56,64},{64,7... | collective-permute-start | bytes 98312 | tf_op jit(solution)/shard_map/while/body/eval_jaxpr/ppermute | solution.py:16
  238.5 8.3 %collective-permute-start = (bf16[1,128,128]{2,1,0:T(8,128)(2,1)S(1)}, bf16[1,128,128]{2,1,0:T(8,128)(2,1)S(1)}, u32[]{:S(2)}, u32[]{:S(2)}) collective-permute-start(bf16[1,128,128]{2,1,0:T(8,128)(2,1)S(1)} %fusion.74), channel_id=1, source_target_pairs={{0,8},{8,16},{16,24},{24,32},{32,40},{40,48},{48,56},{56,64},{64,7... | collective-permute-start | bytes 98312 | tf_op jit(solution)/shard_map/while/body/eval_jaxpr/ppermute | solution.py:16
  246.9 8.3 %collective-permute-start = (bf16[1,128,128]{2,1,0:T(8,128)(2,1)S(1)}, bf16[1,128,128]{2,1,0:T(8,128)(2,1)S(1)}, u32[]{:S(2)}, u32[]{:S(2)}) collective-permute-start(bf16[1,128,128]{2,1,0:T(8,128)(2,1)S(1)} %fusion.74), channel_id=1, source_target_pairs={{0,8},{8,16},{16,24},{24,32},{32,40},{40,48},{48,56},{56,64},{64,7... | collective-permute-start | bytes 98312 | tf_op jit(solution)/shard_map/while/body/eval_jaxpr/ppermute | solution.py:16
  255.2 8.3 %collective-permute-start = (bf16[1,128,128]{2,1,0:T(8,128)(2,1)S(1)}, bf16[1,128,128]{2,1,0:T(8,128)(2,1)S(1)}, u32[]{:S(2)}, u32[]{:S(2)}) collective-permute-start(bf16[1,128,128]{2,1,0:T(8,128)(2,1)S(1)} %fusion.74), channel_id=1, source_target_pairs={{0,8},{8,16},{16,24},{24,32},{32,40},{40,48},{48,56},{56,64},{64,7... | collective-permute-start | bytes 98312 | tf_op jit(solution)/shard_map/while/body/eval_jaxpr/ppermute | solution.py:16
  263.6 8.3 %collective-permute-start = (bf16[1,128,128]{2,1,0:T(8,128)(2,1)S(1)}, bf16[1,128,128]{2,1,0:T(8,128)(2,1)S(1)}, u32[]{:S(2)}, u32[]{:S(2)}) collective-permute-start(bf16[1,128,128]{2,1,0:T(8,128)(2,1)S(1)} %fusion.74), channel_id=1, source_target_pairs={{0,8},{8,16},{16,24},{24,32},{32,40},{40,48},{48,56},{56,64},{64,7... | collective-permute-start | bytes 98312 | tf_op jit(solution)/shard_map/while/body/eval_jaxpr/ppermute | solution.py:16
  271.9 7.8 %collective-permute-start = (bf16[1,128,128]{2,1,0:T(8,128)(2,1)S(1)}, bf16[1,128,128]{2,1,0:T(8,128)(2,1)S(1)}, u32[]{:S(2)}, u32[]{:S(2)}) collective-permute-start(bf16[1,128,128]{2,1,0:T(8,128)(2,1)S(1)} %fusion.74), channel_id=1, source_target_pairs={{0,8},{8,16},{16,24},{24,32},{32,40},{40,48},{48,56},{56,64},{64,7... | collective-permute-start | bytes 98312 | tf_op jit(solution)/shard_map/while/body/eval_jaxpr/ppermute | solution.py:16
  279.8 8.6 %collective-permute-start = (bf16[1,128,128]{2,1,0:T(8,128)(2,1)S(1)}, bf16[1,128,128]{2,1,0:T(8,128)(2,1)S(1)}, u32[]{:S(2)}, u32[]{:S(2)}) collective-permute-start(bf16[1,128,128]{2,1,0:T(8,128)(2,1)S(1)} %fusion.74), channel_id=1, source_target_pairs={{0,8},{8,16},{16,24},{24,32},{32,40},{40,48},{48,56},{56,64},{64,7... | collective-permute-start | bytes 98312 | tf_op jit(solution)/shard_map/while/body/eval_jaxpr/ppermute | solution.py:16
  288.5 8.5 %collective-permute-start = (bf16[1,128,128]{2,1,0:T(8,128)(2,1)S(1)}, bf16[1,128,128]{2,1,0:T(8,128)(2,1)S(1)}, u32[]{:S(2)}, u32[]{:S(2)}) collective-permute-start(bf16[1,128,128]{2,1,0:T(8,128)(2,1)S(1)} %fusion.74), channel_id=1, source_target_pairs={{0,8},{8,16},{16,24},{24,32},{32,40},{40,48},{48,56},{56,64},{64,7... | collective-permute-start | bytes 98312 | tf_op jit(solution)/shard_map/while/body/eval_jaxpr/ppermute | solution.py:16
  297.0 8.0 %collective-permute-start = (bf16[1,128,128]{2,1,0:T(8,128)(2,1)S(1)}, bf16[1,128,128]{2,1,0:T(8,128)(2,1)S(1)}, u32[]{:S(2)}, u32[]{:S(2)}) collective-permute-start(bf16[1,128,128]{2,1,0:T(8,128)(2,1)S(1)} %fusion.74), channel_id=1, source_target_pairs={{0,8},{8,16},{16,24},{24,32},{32,40},{40,48},{48,56},{56,64},{64,7... | collective-permute-start | bytes 98312 | tf_op jit(solution)/shard_map/while/body/eval_jaxpr/ppermute | solution.py:16
  305.1 8.4 %collective-permute-start = (bf16[1,128,128]{2,1,0:T(8,128)(2,1)S(1)}, bf16[1,128,128]{2,1,0:T(8,128)(2,1)S(1)}, u32[]{:S(2)}, u32[]{:S(2)}) collective-permute-start(bf16[1,128,128]{2,1,0:T(8,128)(2,1)S(1)} %fusion.74), channel_id=1, source_target_pairs={{0,8},{8,16},{16,24},{24,32},{32,40},{40,48},{48,56},{56,64},{64,7... | collective-permute-start | bytes 98312 | tf_op jit(solution)/shard_map/while/body/eval_jaxpr/ppermute | solution.py:16
  313.5 8.8 %collective-permute-start = (bf16[1,128,128]{2,1,0:T(8,128)(2,1)S(1)}, bf16[1,128,128]{2,1,0:T(8,128)(2,1)S(1)}, u32[]{:S(2)}, u32[]{:S(2)}) collective-permute-start(bf16[1,128,128]{2,1,0:T(8,128)(2,1)S(1)} %fusion.74), channel_id=1, source_target_pairs={{0,8},{8,16},{16,24},{24,32},{32,40},{40,48},{48,56},{56,64},{64,7... | collective-permute-start | bytes 98312 | tf_op jit(solution)/shard_map/while/body/eval_jaxpr/ppermute | solution.py:16
  322.4 8.4 %collective-permute-start = (bf16[1,128,128]{2,1,0:T(8,128)(2,1)S(1)}, bf16[1,128,128]{2,1,0:T(8,128)(2,1)S(1)}, u32[]{:S(2)}, u32[]{:S(2)}) collective-permute-start(bf16[1,128,128]{2,1,0:T(8,128)(2,1)S(1)} %fusion.74), channel_id=1, source_target_pairs={{0,8},{8,16},{16,24},{24,32},{32,40},{40,48},{48,56},{56,64},{64,7... | collective-permute-start | bytes 98312 | tf_op jit(solution)/shard_map/while/body/eval_jaxpr/ppermute | solution.py:16
  330.8 9.1 %collective-permute-start = (bf16[1,128,128]{2,1,0:T(8,128)(2,1)S(1)}, bf16[1,128,128]{2,1,0:T(8,128)(2,1)S(1)}, u32[]{:S(2)}, u32[]{:S(2)}) collective-permute-start(bf16[1,128,128]{2,1,0:T(8,128)(2,1)S(1)} %fusion.74), channel_id=1, source_target_pairs={{0,8},{8,16},{16,24},{24,32},{32,40},{40,48},{48,56},{56,64},{64,7... | collective-permute-start | bytes 98312 | tf_op jit(solution)/shard_map/while/body/eval_jaxpr/ppermute | solution.py:16
  340.0 8.3 %collective-permute-start = (bf16[1,128,128]{2,1,0:T(8,128)(2,1)S(1)}, bf16[1,128,128]{2,1,0:T(8,128)(2,1)S(1)}, u32[]{:S(2)}, u32[]{:S(2)}) collective-permute-start(bf16[1,128,128]{2,1,0:T(8,128)(2,1)S(1)} %fusion.74), channel_id=1, source_target_pairs={{0,8},{8,16},{16,24},{24,32},{32,40},{40,48},{48,56},{56,64},{64,7... | collective-permute-start | bytes 98312 | tf_op jit(solution)/shard_map/while/body/eval_jaxpr/ppermute | solution.py:16
  348.3 7.7 %collective-permute-start = (bf16[1,128,128]{2,1,0:T(8,128)(2,1)S(1)}, bf16[1,128,128]{2,1,0:T(8,128)(2,1)S(1)}, u32[]{:S(2)}, u32[]{:S(2)}) collective-permute-start(bf16[1,128,128]{2,1,0:T(8,128)(2,1)S(1)} %fusion.74), channel_id=1, source_target_pairs={{0,8},{8,16},{16,24},{24,32},{32,40},{40,48},{48,56},{56,64},{64,7... | collective-permute-start | bytes 98312 | tf_op jit(solution)/shard_map/while/body/eval_jaxpr/ppermute | solution.py:16
  356.1 8.0 %collective-permute-start = (bf16[1,128,128]{2,1,0:T(8,128)(2,1)S(1)}, bf16[1,128,128]{2,1,0:T(8,128)(2,1)S(1)}, u32[]{:S(2)}, u32[]{:S(2)}) collective-permute-start(bf16[1,128,128]{2,1,0:T(8,128)(2,1)S(1)} %fusion.74), channel_id=1, source_target_pairs={{0,8},{8,16},{16,24},{24,32},{32,40},{40,48},{48,56},{56,64},{64,7... | collective-permute-start | bytes 98312 | tf_op jit(solution)/shard_map/while/body/eval_jaxpr/ppermute | solution.py:16
  364.1 8.6 %collective-permute-start = (bf16[1,128,128]{2,1,0:T(8,128)(2,1)S(1)}, bf16[1,128,128]{2,1,0:T(8,128)(2,1)S(1)}, u32[]{:S(2)}, u32[]{:S(2)}) collective-permute-start(bf16[1,128,128]{2,1,0:T(8,128)(2,1)S(1)} %fusion.74), channel_id=1, source_target_pairs={{0,8},{8,16},{16,24},{24,32},{32,40},{40,48},{48,56},{56,64},{64,7... | collective-permute-start | bytes 98312 | tf_op jit(solution)/shard_map/while/body/eval_jaxpr/ppermute | solution.py:16
  372.8 8.2 %collective-permute-start = (bf16[1,128,128]{2,1,0:T(8,128)(2,1)S(1)}, bf16[1,128,128]{2,1,0:T(8,128)(2,1)S(1)}, u32[]{:S(2)}, u32[]{:S(2)}) collective-permute-start(bf16[1,128,128]{2,1,0:T(8,128)(2,1)S(1)} %fusion.74), channel_id=1, source_target_pairs={{0,8},{8,16},{16,24},{24,32},{32,40},{40,48},{48,56},{56,64},{64,7... | collective-permute-start | bytes 98312 | tf_op jit(solution)/shard_map/while/body/eval_jaxpr/ppermute | solution.py:16
  381.0 8.4 %collective-permute-start = (bf16[1,128,128]{2,1,0:T(8,128)(2,1)S(1)}, bf16[1,128,128]{2,1,0:T(8,128)(2,1)S(1)}, u32[]{:S(2)}, u32[]{:S(2)}) collective-permute-start(bf16[1,128,128]{2,1,0:T(8,128)(2,1)S(1)} %fusion.74), channel_id=1, source_target_pairs={{0,8},{8,16},{16,24},{24,32},{32,40},{40,48},{48,56},{56,64},{64,7... | collective-permute-start | bytes 98312 | tf_op jit(solution)/shard_map/while/body/eval_jaxpr/ppermute | solution.py:16
  389.5 8.2 %collective-permute-start = (bf16[1,128,128]{2,1,0:T(8,128)(2,1)S(1)}, bf16[1,128,128]{2,1,0:T(8,128)(2,1)S(1)}, u32[]{:S(2)}, u32[]{:S(2)}) collective-permute-start(bf16[1,128,128]{2,1,0:T(8,128)(2,1)S(1)} %fusion.74), channel_id=1, source_target_pairs={{0,8},{8,16},{16,24},{24,32},{32,40},{40,48},{48,56},{56,64},{64,7... | collective-permute-start | bytes 98312 | tf_op jit(solution)/shard_map/while/body/eval_jaxpr/ppermute | solution.py:16
  397.8 8.3 %collective-permute-start = (bf16[1,128,128]{2,1,0:T(8,128)(2,1)S(1)}, bf16[1,128,128]{2,1,0:T(8,128)(2,1)S(1)}, u32[]{:S(2)}, u32[]{:S(2)}) collective-permute-start(bf16[1,128,128]{2,1,0:T(8,128)(2,1)S(1)} %fusion.74), channel_id=1, source_target_pairs={{0,8},{8,16},{16,24},{24,32},{32,40},{40,48},{48,56},{56,64},{64,7... | collective-permute-start | bytes 98312 | tf_op jit(solution)/shard_map/while/body/eval_jaxpr/ppermute | solution.py:16
  406.1 8.3 %collective-permute-start = (bf16[1,128,128]{2,1,0:T(8,128)(2,1)S(1)}, bf16[1,128,128]{2,1,0:T(8,128)(2,1)S(1)}, u32[]{:S(2)}, u32[]{:S(2)}) collective-permute-start(bf16[1,128,128]{2,1,0:T(8,128)(2,1)S(1)} %fusion.74), channel_id=1, source_target_pairs={{0,8},{8,16},{16,24},{24,32},{32,40},{40,48},{48,56},{56,64},{64,7... | collective-permute-start | bytes 98312 | tf_op jit(solution)/shard_map/while/body/eval_jaxpr/ppermute | solution.py:16
  414.5 8.3 %collective-permute-start = (bf16[1,128,128]{2,1,0:T(8,128)(2,1)S(1)}, bf16[1,128,128]{2,1,0:T(8,128)(2,1)S(1)}, u32[]{:S(2)}, u32[]{:S(2)}) collective-permute-start(bf16[1,128,128]{2,1,0:T(8,128)(2,1)S(1)} %fusion.74), channel_id=1, source_target_pairs={{0,8},{8,16},{16,24},{24,32},{32,40},{40,48},{48,56},{56,64},{64,7... | collective-permute-start | bytes 98312 | tf_op jit(solution)/shard_map/while/body/eval_jaxpr/ppermute | solution.py:16
  (44 other events, 1188.7 us)
Sparse Core Ops, SparseCore 0:
  10.0 75.5 all-gather.4
  88.2 73.7 all-gather.6
  164.6 81.8 all-gather.8
  248.8 82.8 all-gather.10
  454.6 97.9 reduce-scatter.1
where the time goes:
time: 565 us; the launch traced here: 559 us
  waiting for transfers between devices  253 us (45%)
  starting transfers between devices  230 us (41%)
  matrix products  40.5 us (7%)
  other arithmetic  19.2 us (3%)
  between operations  13.4 us (2%)
    ppermute x62, starting transfers between devices, from_behind(): return lax.ppermute(block, axis, route)  230 us
    reduce_scatter x1, waiting for transfers between devices, per_device(): lax.psum_scatter(partial_out.astype(jnp.bfloat16), 'head', scatter_dimens...  98.1 us
    all_gather x1, waiting for transfers between devices, per_device(): value_wide = project(lax.all_gather(wv, 'seq', axis=0, tiled=True))  70.3 us
    all_gather x1, waiting for transfers between devices, per_device(): key_wide = project(lax.all_gather(wk, 'seq', axis=0, tiled=True))  60.1 us
    ppermute x62, waiting for transfers between devices, from_behind(): return lax.ppermute(block, axis, route)  21.9 us
    dot_general x3, matrix products, project(): return jnp.dot(normed, shard_piece, preferred_element_type=jnp.float32)  20.9 us
  transfers between devices with their start and end apart: 67, of which 34 were waited for; matrix products, arithmetic and copies ran while one was open for 9% of the time, Pallas kernels for 0%

commit v1 on v0

--- a/solution.py
+++ b/solution.py
@@ -8,6 +8,14 @@
 KVH = 8
 HD = 128
 SEG = 512
+
+
+def ranges_pass(slab_in, peer_axis):
+    chips = lax.axis_size(peer_axis)
+    in_order = [chips if dev_j == 0 else 1 for dev_j in range(slab_in.ndim)]
+    return lax.all_to_all(
+        jnp.tile(slab_in, in_order), peer_axis, concat_axis=0, split_axis=0, tiled=True
+    )
 
 
 def from_behind(block, axis, distance):
@@ -32,7 +40,7 @@
         return jnp.dot(normed, shard_piece, preferred_element_type=jnp.float32)
 
     query_wide = project(lax.all_gather(wq, "seq", axis=0, tiled=True))
-    key_wide = project(lax.all_gather(wk, "seq", axis=0, tiled=True))
+    key_wide = project(ranges_pass(wk, "seq"))
     value_wide = project(lax.all_gather(wv, "seq", axis=0, tiled=True))
     queries = query_wide.astype(jnp.bfloat16)
     keys_all = key_wide.astype(jnp.bfloat16)

time: 565 us -> 490 us (0.87)
  waiting for transfers between devices: 253 us -> 164 us
  starting transfers between devices: 230 us -> 242 us
    all_gather x1 -> x0, waiting for transfers between devices: 60.1 us -> none  [per_device(): key_wide = project(lax.all_gather(wk, 'seq', axis=0, tiled=True))]
    all_gather x1, waiting for transfers between devices: 70.3 us -> 33.1 us  [per_device(): value_wide = project(lax.all_gather(wv, 'seq', axis=0, tiled=True))]
    all_to_all x0 -> x1, starting transfers between devices: none -> 12 us  [ranges_pass(): lax.all_to_all(jnp.tile(slab_in, in_order), peer_axis, concat_axis=0, spl...]
    all_to_all x0 -> x1, waiting for transfers between devices: none -> 8.47 us  [ranges_pass(): lax.all_to_all(jnp.tile(slab_in, in_order), peer_axis, concat_axis=0, spl...]
  transfers between devices with their start and end apart: 67 -> 67, of which waited for: 34 -> 34; matrix products, arithmetic and copies ran while one was open for 9% -> 11% of each run, Pallas kernels for 0% -> 0%
where the time goes in v1:
time: 490 us; the launch traced here: 484 us
  starting transfers between devices  242 us (49%)
  waiting for transfers between devices  164 us (33%)
  matrix products  40.3 us (8%)
  other arithmetic  19.9 us (4%)
  between operations  13.4 us (3%)
    ppermute x62, starting transfers between devices, from_behind(): return lax.ppermute(block, axis, route)  230 us
    reduce_scatter x1, waiting for transfers between devices, per_device(): lax.psum_scatter(partial_out.astype(jnp.bfloat16), 'head', scatter_dimens...  98.1 us
    all_gather x1, waiting for transfers between devices, per_device(): value_wide = project(lax.all_gather(wv, 'seq', axis=0, tiled=True))  33.1 us
    ppermute x62, waiting for transfers between devices, from_behind(): return lax.ppermute(block, axis, route)  21.9 us
    dot_general x3, matrix products, project(): return jnp.dot(normed, shard_piece, preferred_element_type=jnp.float32)  20.7 us
    all_to_all x1, starting transfers between devices, ranges_pass(): lax.all_to_all(jnp.tile(slab_in, in_order), peer_axis, concat_axis=0, spl...  12 us
    convert_element_type x1, other arithmetic, per_device(): normed = (widened * lax.rsqrt(jnp.mean(widened * widened, axis=-1, keepdi...  10.3 us
  transfers between devices with their start and end apart: 67, of which 34 were waited for; matrix products, arithmetic and copies ran while one was open for 11% of the time, Pallas kernels for 0%

profile of v1, /device:TPU:1, one launch (start us, length us, event | category | flops | bytes accessed | tf_op | source)
XLA Modules:
  0.0 484.2 jit_solution(9521950406188183402)
XLA Ops:
  10.0 12.0 %all-to-all-start = ((bf16[32,128,128]{2,1,0:T(8,128)(2,1)}), bf16[32,128,128]{2,1,0:T(8,128)(2,1)S(1)}, u32[]{:S(2)}, u32[]{:S(2)}) async-start(bf16[32,128,128]{2,1,0:T(8,128)(2,1)} %tile.2), calls=%async_computation | async-start | bytes 2097152 | tf_op jit(solution)/shard_map/all_to_all | solution.py:16
  24.2 5.1 %fusion.3 = f32[1024]{0:T(1024)S(1)} fusion(bf16[1024,4096]{1,0:T(8,128)(2,1)} %param.11), kind=kLoop, calls=%fused_computation.7 | loop fusion | flops 12581888 | bytes 8392704 | tf_op jit(solution)/shard_map/reduce_sum | solution.py:35
  29.3 10.3 %fusion.5 = bf16[1024,4096]{1,0:T(8,128)(2,1)} fusion(bf16[1024,4096]{1,0:T(8,128)(2,1)} %param.11, f32[4096]{0:T(1024)S(1)} %copy-done.2, f32[1024]{0:T(1024)S(1)} %add_rsqrt_fusion), kind=kLoop, calls=%fused_computation.9 | loop fusion | flops 16777216 | bytes 16797696 | tf_op jit(solution)/shard_map/convert_element_type | solution.py:36
  39.6 8.5 %all-to-all-done = bf16[32,128,128]{2,1,0:T(8,128)(2,1)S(1)} async-done(((bf16[32,128,128]{2,1,0:T(8,128)(2,1)}), bf16[32,128,128]{2,1,0:T(8,128)(2,1)S(1)}, u32[]{:S(2)}, u32[]{:S(2)}) %all-to-all-start) | async-done | bytes 1048608 | tf_op jit(solution)/shard_map/all_to_all | solution.py:16
  48.1 5.7 %fusion.38 = (f32[128]{0:T(128)S(1)}, bf16[1024,128]{1,0:T(8,128)(2,1)S(1)}) fusion(bf16[1024,4096]{1,0:T(8,128)(2,1)} %fusion.5, bf16[4096,128]{1,0:T(8,128)(2,1)S(1)} %bitcast.94), kind=kOutput, calls=%fused_computation.57 | convolution fusion | flops 1074659200 | bytes 9699840 | tf_op jit(solution)/shard_map/dot_general | solution.py:40
  54.0 33.1 %all-gather.4.cloned.1.call-done = bf16[4096,128]{1,0:T(8,128)(2,1)} async-done(((bf16[128,128]{1,0:T(8,128)(2,1)}), bf16[4096,128]{1,0:T(8,128)(2,1)}) %all-gather.4.cloned.1.call-update) | async-done | bytes 1048592 | tf_op jit(solution)/shard_map/all_gather | solution.py:44
  87.1 5.9 %convolution_convert_fusion.2 = bf16[1024,128]{1,0:T(8,128)(2,1)S(1)} fusion(bf16[1024,4096]{1,0:T(8,128)(2,1)} %fusion.5, bf16[4096,128]{1,0:T(8,128)(2,1)} %all-gather.4.cloned.1.call-done), kind=kOutput, calls=%fused_computation.32 | convolution fusion | flops 1073872896 | bytes 9699328 | tf_op jit(solution)/shard_map/dot_general | solution.py:40
  94.0 254.0 %while.13 = (s32[]{:T(128)}, f32[1,128,128]{2,1,0:T(8,128)S(1)}, f32[1,128]{1,0:T(1,128)S(1)}, f32[1,128,128]{2,1,0:T(8,128)S(1)}, f32[1,128]{1,0:T(1,128)S(1)}, /*index=5*/s32[]{:T(128)}, s32[]{:T(128)}) while((s32[]{:T(128)}, f32[1,128,128]{2,1,0:T(8,128)S(1)}, f32[1,128]{1,0:T(1,128)S(1)}, f32[1,128,128]{2,1,0:T(8,128)S(1)}, ...), condition=%wide.region_4.5_spmd.clone, body=%wide.region_3.4_spmd.clone.sunk | while | flops 66051 | bytes 396456 | solution.py:70
  96.3 4.0 collective-permute-start.1
  107.3 4.0 collective-permute-start
  122.9 4.0 collective-permute-start
  146.4 4.0 collective-permute-start
  154.9 4.0 collective-permute-start
  158.9 4.0 collective-permute-start.1
  163.7 4.0 collective-permute-start
  172.0 4.0 collective-permute-start
  208.9 4.0 collective-permute-start.1
  225.6 4.0 collective-permute-start.1
  230.4 4.0 collective-permute-start
  234.4 4.1 collective-permute-start.1
  239.2 4.0 collective-permute-start
  243.2 4.0 collective-permute-start.1
  248.0 4.0 collective-permute-start
  259.6 4.8 collective-permute-start.1
  292.9 4.3 collective-permute-start.1
  309.8 4.1 collective-permute-start.1
  326.5 4.0 collective-permute-start.1
  334.8 4.0 collective-permute-start.1
  343.2 4.0 collective-permute-start.1
  348.1 9.1 %convolution_convert_fusion.1 = bf16[1024,512]{1,0:T(8,128)(2,1)S(1)} fusion(bf16[1024,4096]{1,0:T(8,128)(2,1)} %fusion.5, bf16[4096,512]{1,0:T(8,128)(2,1)} %all-gather.6.cloned.1.call-done), kind=kOutput, calls=%fused_computation.31 | convolution fusion | flops 4295491584 | bytes 13631488 | tf_op jit(solution)/shard_map/dot_general | solution.py:40
  370.7 8.9 %convolution_convert_fusion = bf16[1024,4096]{1,0:T(8,128)(2,1)} fusion(bf16[512,4096]{1,0:T(8,128)(2,1)} %all-gather.8.cloned.1.call-done, bf16[128,8,4,128]{3,2,1,0:T(4,128)(2,1)S(1)} %bitcast.95), kind=kOutput, calls=%fused_computation.13 | convolution fusion | flops 4299161600 | bytes 13631488 | tf_op jit(solution)/shard_map/dot_general | solution.py:100
  379.6 98.1 %reduce-scatter.2.cloned.1.call-done = bf16[1024,512]{1,0:T(8,128)(2,1)} async-done(((bf16[1024,4096]{1,0:T(8,128)(2,1)}), bf16[1024,512]{1,0:T(8,128)(2,1)}) %reduce-scatter.2.cloned.1.call-update) | async-done | bytes 1048592 | tf_op jit(solution)/shard_map/reduce_scatter | solution.py:103
  (275 shorter events, 187.5 us)
Async XLA Ops:
  6.5 80.6 %all-gather.4.cloned.1.call-start = ((), (), s32[]{:S(2)}) async-start(), calls=%async_computation.2 | async-start | bytes 1081344 | tf_op jit(solution)/shard_map/all_gather | solution.py:44
  7.3 340.8 %all-gather.6.cloned.1.call-start = ((), (), s32[]{:S(2)}) async-start(), calls=%async_computation.3 | async-start | bytes 4325376 | tf_op jit(solution)/shard_map/all_gather | solution.py:42
  10.0 38.1 %all-to-all-start = ((bf16[32,128,128]{2,1,0:T(8,128)(2,1)}), bf16[32,128,128]{2,1,0:T(8,128)(2,1)S(1)}, u32[]{:S(2)}, u32[]{:S(2)}) async-start(bf16[32,128,128]{2,1,0:T(8,128)(2,1)} %tile.2), calls=%async_computation | async-start | bytes 2097152 | tf_op jit(solution)/shard_map/all_to_all | solution.py:16
  22.0 348.7 %all-gather.8.cloned.1.call-start = ((), (), s32[]{:S(2)}) async-start(), calls=%async_computation.4 | async-start | bytes 4325376 | tf_op jit(solution)/shard_map/all_gather | solution.py:101
  22.8 455.0 %reduce-scatter.2.cloned.1.call-start = ((), (), s32[]{:S(2)}) async-start(), calls=%async_computation.5 | async-start | bytes 9437184 | tf_op jit(solution)/shard_map/reduce_scatter | solution.py:103
  107.3 8.1 %collective-permute-start = (bf16[1,128,128]{2,1,0:T(8,128)(2,1)S(1)}, bf16[1,128,128]{2,1,0:T(8,128)(2,1)S(1)}, u32[]{:S(2)}, u32[]{:S(2)}) collective-permute-start(bf16[1,128,128]{2,1,0:T(8,128)(2,1)S(1)} %fusion.74), channel_id=1, source_target_pairs={{0,8},{8,16},{16,24},{24,32},{32,40},{40,48},{48,56},{56,64},{64,7... | collective-permute-start | bytes 98312 | tf_op jit(solution)/shard_map/while/body/eval_jaxpr/ppermute | solution.py:24
  122.9 8.1 %collective-permute-start = (bf16[1,128,128]{2,1,0:T(8,128)(2,1)S(1)}, bf16[1,128,128]{2,1,0:T(8,128)(2,1)S(1)}, u32[]{:S(2)}, u32[]{:S(2)}) collective-permute-start(bf16[1,128,128]{2,1,0:T(8,128)(2,1)S(1)} %fusion.74), channel_id=1, source_target_pairs={{0,8},{8,16},{16,24},{24,32},{32,40},{40,48},{48,56},{56,64},{64,7... | collective-permute-start | bytes 98312 | tf_op jit(solution)/shard_map/while/body/eval_jaxpr/ppermute | solution.py:24
  131.0 7.8 %collective-permute-start = (bf16[1,128,128]{2,1,0:T(8,128)(2,1)S(1)}, bf16[1,128,128]{2,1,0:T(8,128)(2,1)S(1)}, u32[]{:S(2)}, u32[]{:S(2)}) collective-permute-start(bf16[1,128,128]{2,1,0:T(8,128)(2,1)S(1)} %fusion.74), channel_id=1, source_target_pairs={{0,8},{8,16},{16,24},{24,32},{32,40},{40,48},{48,56},{56,64},{64,7... | collective-permute-start | bytes 98312 | tf_op jit(solution)/shard_map/while/body/eval_jaxpr/ppermute | solution.py:24
  146.4 8.5 %collective-permute-start = (bf16[1,128,128]{2,1,0:T(8,128)(2,1)S(1)}, bf16[1,128,128]{2,1,0:T(8,128)(2,1)S(1)}, u32[]{:S(2)}, u32[]{:S(2)}) collective-permute-start(bf16[1,128,128]{2,1,0:T(8,128)(2,1)S(1)} %fusion.74), channel_id=1, source_target_pairs={{0,8},{8,16},{16,24},{24,32},{32,40},{40,48},{48,56},{56,64},{64,7... | collective-permute-start | bytes 98312 | tf_op jit(solution)/shard_map/while/body/eval_jaxpr/ppermute | solution.py:24
  154.9 8.7 %collective-permute-start = (bf16[1,128,128]{2,1,0:T(8,128)(2,1)S(1)}, bf16[1,128,128]{2,1,0:T(8,128)(2,1)S(1)}, u32[]{:S(2)}, u32[]{:S(2)}) collective-permute-start(bf16[1,128,128]{2,1,0:T(8,128)(2,1)S(1)} %fusion.74), channel_id=1, source_target_pairs={{0,8},{8,16},{16,24},{24,32},{32,40},{40,48},{48,56},{56,64},{64,7... | collective-permute-start | bytes 98312 | tf_op jit(solution)/shard_map/while/body/eval_jaxpr/ppermute | solution.py:24
  163.7 8.3 %collective-permute-start = (bf16[1,128,128]{2,1,0:T(8,128)(2,1)S(1)}, bf16[1,128,128]{2,1,0:T(8,128)(2,1)S(1)}, u32[]{:S(2)}, u32[]{:S(2)}) collective-permute-start(bf16[1,128,128]{2,1,0:T(8,128)(2,1)S(1)} %fusion.74), channel_id=1, source_target_pairs={{0,8},{8,16},{16,24},{24,32},{32,40},{40,48},{48,56},{56,64},{64,7... | collective-permute-start | bytes 98312 | tf_op jit(solution)/shard_map/while/body/eval_jaxpr/ppermute | solution.py:24
  172.0 8.3 %collective-permute-start = (bf16[1,128,128]{2,1,0:T(8,128)(2,1)S(1)}, bf16[1,128,128]{2,1,0:T(8,128)(2,1)S(1)}, u32[]{:S(2)}, u32[]{:S(2)}) collective-permute-start(bf16[1,128,128]{2,1,0:T(8,128)(2,1)S(1)} %fusion.74), channel_id=1, source_target_pairs={{0,8},{8,16},{16,24},{24,32},{32,40},{40,48},{48,56},{56,64},{64,7... | collective-permute-start | bytes 98312 | tf_op jit(solution)/shard_map/while/body/eval_jaxpr/ppermute | solution.py:24
  180.3 8.4 %collective-permute-start = (bf16[1,128,128]{2,1,0:T(8,128)(2,1)S(1)}, bf16[1,128,128]{2,1,0:T(8,128)(2,1)S(1)}, u32[]{:S(2)}, u32[]{:S(2)}) collective-permute-start(bf16[1,128,128]{2,1,0:T(8,128)(2,1)S(1)} %fusion.74), channel_id=1, source_target_pairs={{0,8},{8,16},{16,24},{24,32},{32,40},{40,48},{48,56},{56,64},{64,7... | collective-permute-start | bytes 98312 | tf_op jit(solution)/shard_map/while/body/eval_jaxpr/ppermute | solution.py:24
  188.7 8.3 %collective-permute-start = (bf16[1,128,128]{2,1,0:T(8,128)(2,1)S(1)}, bf16[1,128,128]{2,1,0:T(8,128)(2,1)S(1)}, u32[]{:S(2)}, u32[]{:S(2)}) collective-permute-start(bf16[1,128,128]{2,1,0:T(8,128)(2,1)S(1)} %fusion.74), channel_id=1, source_target_pairs={{0,8},{8,16},{16,24},{24,32},{32,40},{40,48},{48,56},{56,64},{64,7... | collective-permute-start | bytes 98312 | tf_op jit(solution)/shard_map/while/body/eval_jaxpr/ppermute | solution.py:24
  197.1 7.9 %collective-permute-start = (bf16[1,128,128]{2,1,0:T(8,128)(2,1)S(1)}, bf16[1,128,128]{2,1,0:T(8,128)(2,1)S(1)}, u32[]{:S(2)}, u32[]{:S(2)}) collective-permute-start(bf16[1,128,128]{2,1,0:T(8,128)(2,1)S(1)} %fusion.74), channel_id=1, source_target_pairs={{0,8},{8,16},{16,24},{24,32},{32,40},{40,48},{48,56},{56,64},{64,7... | collective-permute-start | bytes 98312 | tf_op jit(solution)/shard_map/while/body/eval_jaxpr/ppermute | solution.py:24
  205.0 8.6 %collective-permute-start = (bf16[1,128,128]{2,1,0:T(8,128)(2,1)S(1)}, bf16[1,128,128]{2,1,0:T(8,128)(2,1)S(1)}, u32[]{:S(2)}, u32[]{:S(2)}) collective-permute-start(bf16[1,128,128]{2,1,0:T(8,128)(2,1)S(1)} %fusion.74), channel_id=1, source_target_pairs={{0,8},{8,16},{16,24},{24,32},{32,40},{40,48},{48,56},{56,64},{64,7... | collective-permute-start | bytes 98312 | tf_op jit(solution)/shard_map/while/body/eval_jaxpr/ppermute | solution.py:24
  213.6 8.3 %collective-permute-start = (bf16[1,128,128]{2,1,0:T(8,128)(2,1)S(1)}, bf16[1,128,128]{2,1,0:T(8,128)(2,1)S(1)}, u32[]{:S(2)}, u32[]{:S(2)}) collective-permute-start(bf16[1,128,128]{2,1,0:T(8,128)(2,1)S(1)} %fusion.74), channel_id=1, source_target_pairs={{0,8},{8,16},{16,24},{24,32},{32,40},{40,48},{48,56},{56,64},{64,7... | collective-permute-start | bytes 98312 | tf_op jit(solution)/shard_map/while/body/eval_jaxpr/ppermute | solution.py:24
  222.0 8.4 %collective-permute-start = (bf16[1,128,128]{2,1,0:T(8,128)(2,1)S(1)}, bf16[1,128,128]{2,1,0:T(8,128)(2,1)S(1)}, u32[]{:S(2)}, u32[]{:S(2)}) collective-permute-start(bf16[1,128,128]{2,1,0:T(8,128)(2,1)S(1)} %fusion.74), channel_id=1, source_target_pairs={{0,8},{8,16},{16,24},{24,32},{32,40},{40,48},{48,56},{56,64},{64,7... | collective-permute-start | bytes 98312 | tf_op jit(solution)/shard_map/while/body/eval_jaxpr/ppermute | solution.py:24
  230.4 8.8 %collective-permute-start = (bf16[1,128,128]{2,1,0:T(8,128)(2,1)S(1)}, bf16[1,128,128]{2,1,0:T(8,128)(2,1)S(1)}, u32[]{:S(2)}, u32[]{:S(2)}) collective-permute-start(bf16[1,128,128]{2,1,0:T(8,128)(2,1)S(1)} %fusion.74), channel_id=1, source_target_pairs={{0,8},{8,16},{16,24},{24,32},{32,40},{40,48},{48,56},{56,64},{64,7... | collective-permute-start | bytes 98312 | tf_op jit(solution)/shard_map/while/body/eval_jaxpr/ppermute | solution.py:24
  239.2 8.7 %collective-permute-start = (bf16[1,128,128]{2,1,0:T(8,128)(2,1)S(1)}, bf16[1,128,128]{2,1,0:T(8,128)(2,1)S(1)}, u32[]{:S(2)}, u32[]{:S(2)}) collective-permute-start(bf16[1,128,128]{2,1,0:T(8,128)(2,1)S(1)} %fusion.74), channel_id=1, source_target_pairs={{0,8},{8,16},{16,24},{24,32},{32,40},{40,48},{48,56},{56,64},{64,7... | collective-permute-start | bytes 98312 | tf_op jit(solution)/shard_map/while/body/eval_jaxpr/ppermute | solution.py:24
  248.0 8.0 %collective-permute-start = (bf16[1,128,128]{2,1,0:T(8,128)(2,1)S(1)}, bf16[1,128,128]{2,1,0:T(8,128)(2,1)S(1)}, u32[]{:S(2)}, u32[]{:S(2)}) collective-permute-start(bf16[1,128,128]{2,1,0:T(8,128)(2,1)S(1)} %fusion.74), channel_id=1, source_target_pairs={{0,8},{8,16},{16,24},{24,32},{32,40},{40,48},{48,56},{56,64},{64,7... | collective-permute-start | bytes 98312 | tf_op jit(solution)/shard_map/while/body/eval_jaxpr/ppermute | solution.py:24
  256.0 9.1 %collective-permute-start = (bf16[1,128,128]{2,1,0:T(8,128)(2,1)S(1)}, bf16[1,128,128]{2,1,0:T(8,128)(2,1)S(1)}, u32[]{:S(2)}, u32[]{:S(2)}) collective-permute-start(bf16[1,128,128]{2,1,0:T(8,128)(2,1)S(1)} %fusion.74), channel_id=1, source_target_pairs={{0,8},{8,16},{16,24},{24,32},{32,40},{40,48},{48,56},{56,64},{64,7... | collective-permute-start | bytes 98312 | tf_op jit(solution)/shard_map/while/body/eval_jaxpr/ppermute | solution.py:24
  265.1 8.2 %collective-permute-start = (bf16[1,128,128]{2,1,0:T(8,128)(2,1)S(1)}, bf16[1,128,128]{2,1,0:T(8,128)(2,1)S(1)}, u32[]{:S(2)}, u32[]{:S(2)}) collective-permute-start(bf16[1,128,128]{2,1,0:T(8,128)(2,1)S(1)} %fusion.74), channel_id=1, source_target_pairs={{0,8},{8,16},{16,24},{24,32},{32,40},{40,48},{48,56},{56,64},{64,7... | collective-permute-start | bytes 98312 | tf_op jit(solution)/shard_map/while/body/eval_jaxpr/ppermute | solution.py:24
  273.4 7.8 %collective-permute-start = (bf16[1,128,128]{2,1,0:T(8,128)(2,1)S(1)}, bf16[1,128,128]{2,1,0:T(8,128)(2,1)S(1)}, u32[]{:S(2)}, u32[]{:S(2)}) collective-permute-start(bf16[1,128,128]{2,1,0:T(8,128)(2,1)S(1)} %fusion.74), channel_id=1, source_target_pairs={{0,8},{8,16},{16,24},{24,32},{32,40},{40,48},{48,56},{56,64},{64,7... | collective-permute-start | bytes 98312 | tf_op jit(solution)/shard_map/while/body/eval_jaxpr/ppermute | solution.py:24
  281.2 8.0 %collective-permute-start = (bf16[1,128,128]{2,1,0:T(8,128)(2,1)S(1)}, bf16[1,128,128]{2,1,0:T(8,128)(2,1)S(1)}, u32[]{:S(2)}, u32[]{:S(2)}) collective-permute-start(bf16[1,128,128]{2,1,0:T(8,128)(2,1)S(1)} %fusion.74), channel_id=1, source_target_pairs={{0,8},{8,16},{16,24},{24,32},{32,40},{40,48},{48,56},{56,64},{64,7... | collective-permute-start | bytes 98312 | tf_op jit(solution)/shard_map/while/body/eval_jaxpr/ppermute | solution.py:24
  289.3 8.6 %collective-permute-start = (bf16[1,128,128]{2,1,0:T(8,128)(2,1)S(1)}, bf16[1,128,128]{2,1,0:T(8,128)(2,1)S(1)}, u32[]{:S(2)}, u32[]{:S(2)}) collective-permute-start(bf16[1,128,128]{2,1,0:T(8,128)(2,1)S(1)} %fusion.74), channel_id=1, source_target_pairs={{0,8},{8,16},{16,24},{24,32},{32,40},{40,48},{48,56},{56,64},{64,7... | collective-permute-start | bytes 98312 | tf_op jit(solution)/shard_map/while/body/eval_jaxpr/ppermute | solution.py:24
  298.0 8.2 %collective-permute-start = (bf16[1,128,128]{2,1,0:T(8,128)(2,1)S(1)}, bf16[1,128,128]{2,1,0:T(8,128)(2,1)S(1)}, u32[]{:S(2)}, u32[]{:S(2)}) collective-permute-start(bf16[1,128,128]{2,1,0:T(8,128)(2,1)S(1)} %fusion.74), channel_id=1, source_target_pairs={{0,8},{8,16},{16,24},{24,32},{32,40},{40,48},{48,56},{56,64},{64,7... | collective-permute-start | bytes 98312 | tf_op jit(solution)/shard_map/while/body/eval_jaxpr/ppermute | solution.py:24
  306.2 8.4 %collective-permute-start = (bf16[1,128,128]{2,1,0:T(8,128)(2,1)S(1)}, bf16[1,128,128]{2,1,0:T(8,128)(2,1)S(1)}, u32[]{:S(2)}, u32[]{:S(2)}) collective-permute-start(bf16[1,128,128]{2,1,0:T(8,128)(2,1)S(1)} %fusion.74), channel_id=1, source_target_pairs={{0,8},{8,16},{16,24},{24,32},{32,40},{40,48},{48,56},{56,64},{64,7... | collective-permute-start | bytes 98312 | tf_op jit(solution)/shard_map/while/body/eval_jaxpr/ppermute | solution.py:24
  314.6 8.2 %collective-permute-start = (bf16[1,128,128]{2,1,0:T(8,128)(2,1)S(1)}, bf16[1,128,128]{2,1,0:T(8,128)(2,1)S(1)}, u32[]{:S(2)}, u32[]{:S(2)}) collective-permute-start(bf16[1,128,128]{2,1,0:T(8,128)(2,1)S(1)} %fusion.74), channel_id=1, source_target_pairs={{0,8},{8,16},{16,24},{24,32},{32,40},{40,48},{48,56},{56,64},{64,7... | collective-permute-start | bytes 98312 | tf_op jit(solution)/shard_map/while/body/eval_jaxpr/ppermute | solution.py:24
  322.9 8.3 %collective-permute-start = (bf16[1,128,128]{2,1,0:T(8,128)(2,1)S(1)}, bf16[1,128,128]{2,1,0:T(8,128)(2,1)S(1)}, u32[]{:S(2)}, u32[]{:S(2)}) collective-permute-start(bf16[1,128,128]{2,1,0:T(8,128)(2,1)S(1)} %fusion.74), channel_id=1, source_target_pairs={{0,8},{8,16},{16,24},{24,32},{32,40},{40,48},{48,56},{56,64},{64,7... | collective-permute-start | bytes 98312 | tf_op jit(solution)/shard_map/while/body/eval_jaxpr/ppermute | solution.py:24
  331.2 8.3 %collective-permute-start = (bf16[1,128,128]{2,1,0:T(8,128)(2,1)S(1)}, bf16[1,128,128]{2,1,0:T(8,128)(2,1)S(1)}, u32[]{:S(2)}, u32[]{:S(2)}) collective-permute-start(bf16[1,128,128]{2,1,0:T(8,128)(2,1)S(1)} %fusion.74), channel_id=1, source_target_pairs={{0,8},{8,16},{16,24},{24,32},{32,40},{40,48},{48,56},{56,64},{64,7... | collective-permute-start | bytes 98312 | tf_op jit(solution)/shard_map/while/body/eval_jaxpr/ppermute | solution.py:24
  339.6 8.3 %collective-permute-start = (bf16[1,128,128]{2,1,0:T(8,128)(2,1)S(1)}, bf16[1,128,128]{2,1,0:T(8,128)(2,1)S(1)}, u32[]{:S(2)}, u32[]{:S(2)}) collective-permute-start(bf16[1,128,128]{2,1,0:T(8,128)(2,1)S(1)} %fusion.74), channel_id=1, source_target_pairs={{0,8},{8,16},{16,24},{24,32},{32,40},{40,48},{48,56},{56,64},{64,7... | collective-permute-start | bytes 98312 | tf_op jit(solution)/shard_map/while/body/eval_jaxpr/ppermute | solution.py:24
  (43 other events, 1337.8 us)
Sparse Core Ops, SparseCore 0:
  9.9 77.1 all-gather.3
  89.7 81.8 all-gather.5
  174.1 82.8 all-gather.7
  379.8 97.9 reduce-scatter.1
